TPU v7x, 256 devices: a whole 4x4x8 slice. The times are simulated.
256 devices in a mesh: tm: 16 (over y_lo, x, core), col: 16 (over z, y_hi).
Axes of the slice: x: 4, y: 4 (y_hi: 2, y_lo: 2; y = y_hi * 2 + y_lo), z: 8, core: 2. Of those that a mesh axis runs over, the one named last changes fastest.
Arguments:
- panel: bfloat16 [1024, 131072], P('col', 'tm'), may hold values from -60 to 60
- response: float32 [131072], replicated, may hold values from 0.25 to 2.5
Outputs:
- normal: float32 [1024, 1024], P('col', 'tm')
All inputs are finite; a program needn't handle non-finite values.
Results may differ from a plain program's by a relative error of at most 0.0015.
Values may be sent and summed in bfloat16 or wider, within the bound.
No kernel may reach another device: no remote copies, remote signals or barrier semaphores. Data moves between devices by JAX's collectives and lax.ppermute only.
A program may use at most 64 MiB of HBM per device.

v0:
```python
import math
import jax
import jax.numpy as jnp
from jax import lax
from jax.sharding import PartitionSpec as P

EPOCHS = 131072


def angle_tables(row_count, col_count, length):
    row_index = jnp.arange(row_count, dtype=jnp.int32)[:, None]
    col_index = jnp.arange(col_count, dtype=jnp.int32)[None, :]
    phase_index = row_index * col_index % length
    angle = phase_index.astype(jnp.float32) * (2.0 * math.pi / length)
    return (jnp.cos(angle), jnp.sin(angle))


def mixed(form, left, right):
    return jnp.einsum(form, left, right, precision=lax.Precision.HIGHEST)


def split_table(table):
    upper = table.astype(jnp.bfloat16)
    lower = (table - upper.astype(jnp.float32)).astype(jnp.bfloat16)
    return (upper, lower)


def exact_first(table, values):
    upper, lower = split_table(table)
    first = jnp.einsum("kja,jban->kbn", upper, values, preferred_element_type=jnp.float32)
    return first + jnp.einsum("kja,jban->kbn", lower, values, preferred_element_type=jnp.float32)


def whiten_series(series, tables):
    outer_cos, outer_sin, twist_cos, twist_sin, inner_cos, inner_sin, gain_grid = tables
    block_count, item_count, block_len = series.shape
    inner_len = inner_cos.shape[0]
    steps_per_block = block_len // inner_len
    outer_len = block_count * steps_per_block
    values = series.reshape(block_count, item_count, steps_per_block, inner_len)
    fold_cos = outer_cos.reshape(outer_len, block_count, steps_per_block)
    fold_sin = outer_sin.reshape(outer_len, block_count, steps_per_block)
    first_re = exact_first(fold_cos, values)
    first_im = -exact_first(fold_sin, values)
    turn_cos = twist_cos[:, None, :]
    turn_sin = twist_sin[:, None, :]
    turned_re = first_re * turn_cos + first_im * turn_sin
    turned_im = first_im * turn_cos - first_re * turn_sin
    spec_re = mixed("kbn,nl->kbl", turned_re, inner_cos) + mixed(
        "kbn,nl->kbl", turned_im, inner_sin
    )
    spec_im = mixed("kbn,nl->kbl", turned_im, inner_cos) - mixed(
        "kbn,nl->kbl", turned_re, inner_sin
    )
    weight = gain_grid[:, None, :]
    filt_re = spec_re * weight
    filt_im = spec_im * weight
    back_re = mixed("kbl,ln->kbn", filt_re, inner_cos) - mixed("kbl,ln->kbn", filt_im, inner_sin)
    back_im = mixed("kbl,ln->kbn", filt_im, inner_cos) + mixed("kbl,ln->kbn", filt_re, inner_sin)
    untw_re = back_re * turn_cos - back_im * turn_sin
    untw_im = back_im * turn_cos + back_re * turn_sin
    spread_cos = outer_cos.reshape(block_count, steps_per_block, outer_len)
    spread_sin = outer_sin.reshape(block_count, steps_per_block, outer_len)
    result = mixed("jak,kbn->jban", spread_cos, untw_re) - mixed(
        "jak,kbn->jban", spread_sin, untw_im
    )
    result = result * (1.0 / (outer_len * inner_len))
    return result.reshape(block_count, item_count, block_len).astype(jnp.bfloat16)


def on_device(panel, response):
    col_rows, epoch_count = panel.shape
    tm_count = lax.axis_size("tm")
    total_len = tm_count * epoch_count
    inner_len = math.gcd(256, epoch_count)
    outer_len = total_len // inner_len
    outer_cos, outer_sin = angle_tables(outer_len, outer_len, outer_len)
    twist_cos, twist_sin = angle_tables(outer_len, inner_len, total_len)
    inner_cos, inner_sin = angle_tables(inner_len, inner_len, inner_len)
    gain_grid = response.reshape(inner_len, outer_len).T
    tables = (outer_cos, outer_sin, twist_cos, twist_sin, inner_cos, inner_sin, gain_grid)
    grouped = panel.reshape(tm_count, col_rows // tm_count, epoch_count)
    filtered = whiten_series(
        lax.all_to_all(grouped, "tm", split_axis=0, concat_axis=0, tiled=True), tables
    )
    landed = lax.all_to_all(filtered, "tm", split_axis=0, concat_axis=0, tiled=True)
    whitened = landed.reshape(col_rows, epoch_count)
    partial_sum = lax.dot_general(
        whitened,
        lax.all_gather(whitened, "col", axis=0, tiled=True),
        (((1,), (1,)), ((), ())),
        preferred_element_type=jnp.float32,
    )
    summed = lax.psum_scatter(partial_sum, "tm", scatter_dimension=1, tiled=True)
    return summed / EPOCHS


def solution(mesh):
    in_specs = (P("col", "tm"), P())
    out_specs = P("col", "tm")
    return jax.shard_map(
        on_device, mesh=mesh, in_specs=in_specs, out_specs=out_specs, check_vma=False
    )
```

profile of v0, /device:TPU:32, one launch (start us, length us, event | category | flops | bytes accessed | tf_op | source)
XLA Modules:
  0.0 416.5 jit_solution(12158881425810183495)
XLA Ops:
  6.5 2.3 reshape.89
  8.8 5.4 %all-to-all-start = ((bf16[16,4,8192]{2,1,0:T(4,128)(2,1)}), bf16[16,4,8192]{2,1,0:T(4,128)(2,1)S(1)}, u32[]{:S(2)}, u32[]{:S(2)}) async-start(bf16[16,4,8192]{2,1,0:T(4,128)(2,1)} %reshape.89), calls=%async_computation | async-start | bytes 2097152 | tf_op jit(solution)/shard_map/all_to_all | solution.py:84
  14.2 0.0 all-gather.2.cloned.1.call-start
  14.3 0.1 reshape.91
  14.4 0.2 copy.8
  14.6 2.1 fusion.79
  16.7 14.0 %all-to-all-done = bf16[16,4,8192]{2,1,0:T(4,128)(2,1)S(1)} async-done(((bf16[16,4,8192]{2,1,0:T(4,128)(2,1)}), bf16[16,4,8192]{2,1,0:T(4,128)(2,1)S(1)}, u32[]{:S(2)}, u32[]{:S(2)}) %all-to-all-start) | async-done | bytes 1048608 | tf_op jit(solution)/shard_map/all_to_all | solution.py:84
  30.7 2.0 reshape.107
  32.7 5.7 %fusion.43 = f32[512,4,256,1]{2,0,1,3:T(8,128)S(1)} fusion(bf16[16,4,32,256]{3,2,1,0:T(8,128)(2,1)} %reshape.107, s32[16,32]{1,0:T(8,128)S(1)} %multiply_add_fusion.3), kind=kOutput, calls=%fused_computation.58 | convolution fusion | flops 540803072 | bytes 3147776 | tf_op jit(solution)/shard_map/kja,jban->kbn/dot_general | solution.py:30
  38.4 4.4 %fusion.45 = f32[512,4,256,1]{2,0,1,3:T(8,128)S(1)} fusion(bf16[16,4,32,256]{3,2,1,0:T(8,128)(2,1)S(1)} %copy-done.1, s32[16,32]{1,0:T(8,128)S(1)} %multiply_add_fusion.3), kind=kOutput, calls=%fused_computation.60 | convolution fusion | flops 540803072 | bytes 3147776 | tf_op jit(solution)/shard_map/kja,jban->kbn/dot_general | solution.py:30
  42.8 4.6 %fusion = f32[512,4,256]{2,0,1:T(8,128)S(1)} fusion(f32[512,4,256,1]{2,0,1,3:T(8,128)S(1)} %fusion.43, bf16[16,4,32,256]{3,2,1,0:T(8,128)(2,1)S(1)} %copy-done.1, s32[16,32]{1,0:T(8,128)S(1)} %multiply_add_fusion.3), kind=kOutput, calls=%fused_computation.1 | convolution fusion | flops 542638080 | bytes 5244928 | tf_op jit(solution)/shard_map/kja,jban->kbn/dot_general | solution.py:31
  47.4 4.4 %bitcast_add_fusion.1 = f32[512,4,256]{2,0,1:T(8,128)S(1)} fusion(f32[512,4,256,1]{2,0,1,3:T(8,128)S(1)} %fusion.45, bf16[16,4,32,256]{3,2,1,0:T(8,128)(2,1)S(1)} %copy-done.1, s32[16,32]{1,0:T(8,128)S(1)} %multiply_add_fusion.3), kind=kOutput, calls=%fused_computation.2 | convolution fusion | flops 542113792 | bytes 5244928 | tf_op jit(solution)/shard_map/kja,jban->kbn/dot_general | solution.py:31
  51.9 3.1 fusion.71
  54.9 3.1 fusion.75
  58.0 3.4 subtract_multiply_fusion
  61.4 2.8 fusion.69
  64.3 3.2 add_multiply_fusion
  67.4 2.8 fusion.73
  70.3 3.3 convolution_add_fusion
  73.6 2.9 convolution_subtract_fusion
  76.6 7.8 %fusion.1 = f32[4,256,16,32]{1,3,2,0:T(8,128)S(1)} fusion(f32[512,4,256]{2,0,1:T(8,128)S(1)} %convolution_subtract_fusion, f32[512,4,256]{2,0,1:T(8,128)S(1)} %convolution_add_fusion, f32[512,256]{1,0:T(8,128)S(1)} %get-tuple-element.5, f32[512,256]{1,0:T(8,128)S(1)} %get-tuple-element.6, s32[16,32]{1,0:T(8,128)S(1)} %multiply_add_fusion.3), kind=kOutput, calls=%fused_computation.3 | convolution fusion | flops 3226468352 | bytes 7342080 | tf_op jit(solution)/shard_map/jak,kbn->jban/dot_general | solution.py:19
  84.4 7.7 %fusion.13 = bf16[16,4,32,256]{3,2,0,1:T(8,128)(2,1)S(1)} fusion(f32[4,256,16,32]{1,3,2,0:T(8,128)S(1)} %fusion.1, f32[512,4,256]{2,0,1:T(8,128)S(1)} %convolution_add_fusion, f32[512,4,256]{2,0,1:T(8,128)S(1)} %convolution_subtract_fusion, f32[512,256]{1,0:T(8,128)S(1)} %get-tuple-element.5, f32[512,256]{1,0:T(8,128)S(1)} %get-tuple-element.6, ...), kind=kOutput, calls=%fused_computation.26 | convolution fusion | flops 3228041216 | bytes 8390656 | tf_op jit(solution)/shard_map/jak,kbn->jban/dot_general | solution.py:19
  92.1 0.5 convert_element_type.101
  92.7 0.8 copy.9
  93.5 19.1 %all_to_all.10 = bf16[16,4,8192]{2,1,0:T(4,128)(2,1)S(1)} all-to-all(bf16[16,4,8192]{2,1,0:T(4,128)(2,1)S(1)} %copy.9), channel_id=1, replica_groups=mesh['tm'=16,'col'=16] {'tm'}, dimensions={0} | all-to-all | bytes 2097152 | tf_op jit(solution)/shard_map/all_to_all | solution.py:86
  112.6 1.1 reshape.92
  113.7 0.0 reduce-scatter.4.cloned.1.call-start
  113.7 222.7 %all-gather.2.cloned.1.call-done = bf16[1024,8192]{1,0:T(8,128)(2,1)} async-done(((bf16[64,8192]{1,0:T(8,128)(2,1)}), bf16[1024,8192]{1,0:T(8,128)(2,1)}) %all-gather.2.cloned.1.call-update) | async-done | bytes 16777232 | tf_op jit(solution)/shard_map/all_gather | solution.py:90
  336.5 8.9 %convolution_bitcast_fusion = f32[1024,64]{1,0:T(8,128)} fusion(bf16[64,8192]{1,0:T(8,128)(2,1)S(1)} %copy-done, bf16[1024,8192]{1,0:T(8,128)(2,1)} %all-gather.2.cloned.1.call-done), kind=kOutput, calls=%fused_computation.27 | convolution fusion | flops 1073741824 | bytes 18087936
  345.4 62.6 %reduce-scatter.4.cloned.1.call-done = f32[64,64]{1,0:T(8,128)} async-done(((f32[1024,64]{1,0:T(8,128)}), f32[64,64]{1,0:T(8,128)}) %reduce-scatter.4.cloned.1.call-update) | async-done | bytes 16400
  408.0 0.8 copy.18
  408.9 0.6 broadcast_multiply_fusion
  (9 shorter events, 0.1 us)
Async XLA Ops:
  6.5 7.8 %copy-start.2 = (f32[131072]{0:T(1024)S(1)}, f32[131072]{0:T(1024)}, u32[]{:S(2)}) copy-start(f32[131072]{0:T(1024)} %param.3) | copy-start | bytes 1572868
  8.8 21.9 %all-to-all-start = ((bf16[16,4,8192]{2,1,0:T(4,128)(2,1)}), bf16[16,4,8192]{2,1,0:T(4,128)(2,1)S(1)}, u32[]{:S(2)}, u32[]{:S(2)}) async-start(bf16[16,4,8192]{2,1,0:T(4,128)(2,1)} %reshape.89), calls=%async_computation | async-start | bytes 2097152 | tf_op jit(solution)/shard_map/all_to_all | solution.py:84
  14.2 322.2 %all-gather.2.cloned.1.call-start = ((), (), s32[]{:S(2)}) async-start(), calls=%async_computation.3 | async-start | bytes 17825792 | tf_op jit(solution)/shard_map/all_gather | solution.py:90
  32.7 5.7 %copy-start.1 = (bf16[16,4,32,256]{3,2,1,0:T(8,128)(2,1)S(1)}, bf16[16,4,32,256]{3,2,1,0:T(8,128)(2,1)}, u32[]{:S(2)}) copy-start(bf16[16,4,32,256]{3,2,1,0:T(8,128)(2,1)} %reshape.107) | copy-start | bytes 3145732
  113.6 222.8 %copy-start = (bf16[64,8192]{1,0:T(8,128)(2,1)S(1)}, bf16[64,8192]{1,0:T(8,128)(2,1)}, u32[]{:S(2)}) copy-start(bf16[64,8192]{1,0:T(8,128)(2,1)} %reshape.92) | copy-start | bytes 3145732
  113.7 294.4 %reduce-scatter.4.cloned.1.call-start = ((), (), s32[]{:S(2)}) async-start(), calls=%async_computation.4 | async-start | bytes 557056
Sparse Core Ops, SparseCore 0:
  113.8 222.6 all-gather.1
  345.5 62.4 reduce-scatter.3
where the time goes:
time: 420 us; the launch traced here: 417 us
  waiting for transfers between devices  299 us (71%)
  matrix products  68.2 us (16%)
  blocking collectives  19.1 us (5%)
  between operations  13.8 us (3%)
  local copies, waits for them, and re-layouts  7.8 us (2%)
  starting transfers between devices  5.5 us (1%)
    all_gather x1, waiting for transfers between devices, on_device(): lax.all_gather(whitened, 'col', axis=0, tiled=True)  223 us
    unnamed x3, waiting for transfers between devices  62.7 us
    dot_general x10, matrix products, mixed(): return jnp.einsum(form, left, right, precision=lax.Precision.HIGHEST)  40.2 us
    all_to_all x1, blocking collectives, on_device(): lax.all_to_all(filtered, 'tm', split_axis=0, concat_axis=0, tiled=True)  19.1 us
    all_to_all x1, waiting for transfers between devices, on_device(): lax.all_to_all(grouped, 'tm', split_axis=0, concat_axis=0, tiled=True)  14 us
    dot_general x2, matrix products, exact_first(): jnp.einsum('kja,jban->kbn', upper, values, preferred_element_type=jnp.flo...  10.1 us
    dot_general x2, matrix products, exact_first(): jnp.einsum('kja,jban->kbn', lower, values, preferred_element_type=jnp.flo...  9.04 us
    unnamed x1, matrix products  8.9 us
  transfers between devices with their start and end apart: 3, of which 3 were waited for; matrix products, arithmetic and copies ran while one was open for 1% of the time, Pallas kernels for 0%

commit v1 on v0

--- a/solution.py
+++ b/solution.py
@@ -87,7 +87,9 @@
     whitened = landed.reshape(col_rows, epoch_count)
     partial_sum = lax.dot_general(
         whitened,
-        lax.all_gather(whitened, "col", axis=0, tiled=True),
+        jnp.concatenate(
+            lax.all_to_all(jnp.stack([whitened] * lax.axis_size("col")), "col", 0, 0), axis=0
+        ),
         (((1,), (1,)), ((), ())),
         preferred_element_type=jnp.float32,
     )

time: 420 us -> 566 us (1.35)
  blocking collectives: 19.1 us -> 395 us
  waiting for transfers between devices: 299 us -> 72.7 us
    all_to_all x0 -> x1, blocking collectives: none -> 376 us  [on_device(): lax.all_to_all(jnp.stack([whitened] * lax.axis_size('col')), 'col', 0, 0)]
    all_gather x1 -> x0, waiting for transfers between devices: 223 us -> none  [on_device(): lax.all_gather(whitened, 'col', axis=0, tiled=True)]
    unnamed x3 -> x2, waiting for transfers between devices: 62.7 us -> 58.7 us
  transfers between devices with their start and end apart: 3 -> 2, of which waited for: 3 -> 2; matrix products, arithmetic and copies ran while one was open for 1% -> 0% of each run, Pallas kernels for 0% -> 0%
where the time goes in v1:
time: 566 us; the launch traced here: 563 us
  blocking collectives  395 us (70%)
  waiting for transfers between devices  72.7 us (13%)
  matrix products  64.9 us (11%)
  between operations  13.8 us (2%)
  local copies, waits for them, and re-layouts  8.52 us (2%)
    all_to_all x1, blocking collectives, on_device(): lax.all_to_all(jnp.stack([whitened] * lax.axis_size('col')), 'col', 0, 0)  376 us
    unnamed x2, waiting for transfers between devices  58.7 us
    dot_general x10, matrix products, mixed(): return jnp.einsum(form, left, right, precision=lax.Precision.HIGHEST)  40.1 us
    all_to_all x1, blocking collectives, on_device(): lax.all_to_all(filtered, 'tm', split_axis=0, concat_axis=0, tiled=True)  19.1 us
    all_to_all x1, waiting for transfers between devices, on_device(): lax.all_to_all(grouped, 'tm', split_axis=0, concat_axis=0, tiled=True)  14 us
  transfers between devices with their start and end apart: 2, of which 2 were waited for; matrix products, arithmetic and copies ran while one was open for 0% of the time, Pallas kernels for 0%

profile of v1, /device:TPU:32, one launch (start us, length us, event | category | flops | bytes accessed | tf_op | source)
XLA Modules:
  0.0 562.9 jit_solution(6022214569599451113)
XLA Ops:
  6.5 2.3 reshape.94
  8.8 5.4 all-to-all-start
  14.3 0.0 reduce-scatter.4.cloned.1.call-start
  14.3 0.1 reshape.96
  14.4 0.2 copy.8
  14.6 2.1 fusion.79
  16.7 14.0 %all-to-all-done = bf16[16,4,8192]{2,1,0:T(4,128)(2,1)S(1)} async-done(((bf16[16,4,8192]{2,1,0:T(4,128)(2,1)}), bf16[16,4,8192]{2,1,0:T(4,128)(2,1)S(1)}, u32[]{:S(2)}, u32[]{:S(2)}) %all-to-all-start) | async-done | bytes 1048608 | tf_op jit(solution)/shard_map/all_to_all | solution.py:84
  30.7 1.8 reshape.113
  32.5 5.7 %fusion.43 = f32[512,4,256,1]{2,0,1,3:T(8,128)S(1)} fusion(bf16[16,4,32,256]{3,2,1,0:T(8,128)(2,1)} %reshape.113, s32[16,32]{1,0:T(8,128)S(1)} %multiply_add_fusion.3), kind=kOutput, calls=%fused_computation.58 | convolution fusion | flops 540803072 | bytes 3147776 | tf_op jit(solution)/shard_map/kja,jban->kbn/dot_general | solution.py:30
  38.3 4.4 fusion.45
  42.7 5.0 fusion
  47.6 4.4 bitcast_add_fusion.1
  52.1 3.1 fusion.71
  55.1 3.1 fusion.75
  58.2 3.3 subtract_multiply_fusion
  61.6 2.8 fusion.69
  64.4 3.2 add_multiply_fusion
  67.6 2.8 fusion.73
  70.4 3.1 convolution_add_fusion
  73.5 2.9 convolution_subtract_fusion
  76.5 8.0 %fusion.1 = f32[4,256,16,32]{1,3,2,0:T(8,128)S(1)} fusion(f32[512,4,256]{2,0,1:T(8,128)S(1)} %convolution_subtract_fusion, f32[512,4,256]{2,0,1:T(8,128)S(1)} %convolution_add_fusion, f32[512,256]{1,0:T(8,128)S(1)} %get-tuple-element.5, f32[512,256]{1,0:T(8,128)S(1)} %get-tuple-element.6, s32[16,32]{1,0:T(8,128)S(1)} %multiply_add_fusion.3), kind=kOutput, calls=%fused_computation.3 | convolution fusion | flops 3226468352 | bytes 7342080 | tf_op jit(solution)/shard_map/jak,kbn->jban/dot_general | solution.py:19
  84.5 7.7 %fusion.13 = bf16[16,4,32,256]{3,2,0,1:T(8,128)(2,1)S(1)} fusion(f32[4,256,16,32]{1,3,2,0:T(8,128)S(1)} %fusion.1, f32[512,4,256]{2,0,1:T(8,128)S(1)} %convolution_add_fusion, f32[512,4,256]{2,0,1:T(8,128)S(1)} %convolution_subtract_fusion, f32[512,256]{1,0:T(8,128)S(1)} %get-tuple-element.5, f32[512,256]{1,0:T(8,128)S(1)} %get-tuple-element.6, ...), kind=kOutput, calls=%fused_computation.26 | convolution fusion | flops 3228041216 | bytes 8390656 | tf_op jit(solution)/shard_map/jak,kbn->jban/dot_general | solution.py:19
  92.2 0.5 convert_element_type.101
  92.8 0.8 copy.9
  93.6 19.1 %all_to_all.15 = bf16[16,4,8192]{2,1,0:T(4,128)(2,1)S(1)} all-to-all(bf16[16,4,8192]{2,1,0:T(4,128)(2,1)S(1)} %copy.9), channel_id=1, replica_groups=mesh['tm'=16,'col'=16] {'tm'}, dimensions={0} | all-to-all | bytes 2097152 | tf_op jit(solution)/shard_map/all_to_all | solution.py:86
  112.7 0.3 reshape.97
  112.9 1.7 stack.3
  114.7 375.8 %all_to_all.16 = bf16[16,64,8192]{2,1,0:T(8,128)(2,1)S(1)} all-to-all(bf16[16,64,8192]{2,1,0:T(8,128)(2,1)S(1)} %stack.3), channel_id=1, replica_groups=mesh['tm'=16,'col'=16] {'col'}, dimensions={0} | all-to-all | bytes 33554432 | tf_op jit(solution)/shard_map/all_to_all | solution.py:91
  490.5 5.3 convolution_bitcast_fusion
  495.8 58.7 %reduce-scatter.4.cloned.1.call-done = f32[64,64]{1,0:T(8,128)} async-done(((f32[1024,64]{1,0:T(8,128)}), f32[64,64]{1,0:T(8,128)}) %reduce-scatter.4.cloned.1.call-update) | async-done | bytes 16400
  554.4 0.8 copy.18
  555.3 0.6 broadcast_multiply_fusion
  (6 shorter events, 0.0 us)
Async XLA Ops:
  6.5 7.8 %copy-start.1 = (f32[131072]{0:T(1024)S(1)}, f32[131072]{0:T(1024)}, u32[]{:S(2)}) copy-start(f32[131072]{0:T(1024)} %param.3) | copy-start | bytes 1572868
  8.8 21.9 %all-to-all-start = ((bf16[16,4,8192]{2,1,0:T(4,128)(2,1)}), bf16[16,4,8192]{2,1,0:T(4,128)(2,1)S(1)}, u32[]{:S(2)}, u32[]{:S(2)}) async-start(bf16[16,4,8192]{2,1,0:T(4,128)(2,1)} %reshape.94), calls=%async_computation | async-start | bytes 2097152 | tf_op jit(solution)/shard_map/all_to_all | solution.py:84
  14.3 540.2 %reduce-scatter.4.cloned.1.call-start = ((), (), s32[]{:S(2)}) async-start(), calls=%async_computation.4 | async-start | bytes 557056
  32.5 5.7 %copy-start = (bf16[16,4,32,256]{3,2,1,0:T(8,128)(2,1)S(1)}, bf16[16,4,32,256]{3,2,1,0:T(8,128)(2,1)}, u32[]{:S(2)}) copy-start(bf16[16,4,32,256]{3,2,1,0:T(8,128)(2,1)} %reshape.113) | copy-start | bytes 3145732
Sparse Core Ops, SparseCore 0:
  495.9 58.4 reduce-scatter.3
